TPU v7x, 128 devices: a whole 4x4x4 slice. The times are simulated.
128 devices in a mesh: range: 16 (over z, y), doppler: 8 (over x, core).
Axes of the slice: x: 4, y: 4, z: 4, core: 2. Of those that a mesh axis runs over, the one named last changes fastest.
Arguments:
- snapshots: bfloat16 [128, 16384, 384], P(None, ('range', 'doppler')), may hold values from -24 to 24
- steering: bfloat16 [128, 384, 256], P(('range', 'doppler')), may hold values from -0.3125 to 0.3125
- train_list: int32 [128, 128], P(('range', 'doppler')), may hold values from 0 to 127, each once within a row
- train_count: int32 [128], P(('range', 'doppler')), may hold values from 42 to 128, as said below
Outputs:
- beam_output: bfloat16 [128, 16384, 256], P(None, ('range', 'doppler'))
Inputs may be any that keep to these rules, and one draw needn't show every extreme that they name: `train_count`: some bin trains on all 128 blocks and some bin on 42.
All inputs are finite; a program needn't handle non-finite values.
Results may differ from a plain program's by a relative error of at most 0.0052.
Values may be sent and summed in bfloat16 or wider, within the bound.
A program may use at most 128 MiB of HBM per device.

v0:
```python
import jax
import jax.numpy as jnp
from jax import lax
from jax.sharding import PartitionSpec as P

BLOCK = 128
LOADING = 0.1


def selection(train_list, train_count):
    block_total = train_list.shape[1]
    position = lax.broadcasted_iota(jnp.int32, (1, block_total, 1), 1)
    block_ids = lax.broadcasted_iota(jnp.int32, (1, 1, block_total), 2)
    matches = (train_list[:, :, None] == block_ids) & (position < train_count[:, None, None])
    return jnp.sum(matches.astype(jnp.int32), axis=1)


def solve_one(factor, rhs_block):
    inner = lax.linalg.triangular_solve(factor, rhs_block, left_side=True, lower=True)
    return lax.linalg.triangular_solve(factor, inner, left_side=True, lower=True, transpose_a=True)


def adapt(own_snaps, train_list, train_count, steering):
    own_bins, gate_total, channels = own_snaps.shape
    block_total = train_list.shape[1]
    chosen = selection(train_list, train_count)
    blocks = own_snaps.reshape(own_bins, block_total, gate_total // block_total, channels)
    masked = blocks * chosen.astype(own_snaps.dtype)[:, :, None, None]
    gram_sum = jnp.einsum("bnrd,bnre->bde", masked, blocks, preferred_element_type=jnp.float32)
    scale = (BLOCK * train_count).astype(jnp.float32)
    covariance = (
        gram_sum / scale[:, None, None] + LOADING * jnp.eye(channels, dtype=jnp.float32)[None]
    )
    factor = jnp.linalg.cholesky(covariance)
    steer_full = steering.astype(jnp.float32)
    solved = jax.vmap(solve_one)(factor, steer_full)
    response = jnp.sum(steer_full * solved, axis=1)
    return (solved / response[:, None, :]).astype(jnp.bfloat16)


def body(snapshots, steering, train_list, train_count):
    bin_total, gate_rows, channels = snapshots.shape
    own_bins = steering.shape[0]
    devices = bin_total // own_bins
    outgoing = snapshots.reshape(devices, own_bins, gate_rows, channels)
    arrived = lax.all_to_all(
        outgoing, ("range", "doppler"), split_axis=0, concat_axis=0, tiled=True
    )
    own_snaps = jnp.moveaxis(arrived, 1, 0).reshape(own_bins, devices * gate_rows, channels)
    weights = adapt(own_snaps, train_list, train_count, steering)
    return jnp.einsum(
        "bgd,bde->bge",
        snapshots,
        lax.all_gather(weights, ("range", "doppler"), axis=0, tiled=True),
        preferred_element_type=jnp.float32,
    ).astype(jnp.bfloat16)


def solution(mesh):
    placed = (
        P(None, ("range", "doppler"), None),
        P(("range", "doppler"), None, None),
        P(("range", "doppler"), None),
        P(("range", "doppler")),
    )
    return jax.shard_map(
        body,
        mesh=mesh,
        in_specs=placed,
        out_specs=P(None, ("range", "doppler"), None),
        check_vma=False,
    )
```

profile of v0, /device:TPU:1, one launch (start us, length us, event | category | flops | bytes accessed | tf_op | source)
XLA Modules:
  0.0 431.1 jit_solution(15140216038816594535)
XLA Ops:
  6.5 0.0 copy-start.1
  6.5 11.9 %all-to-all-start = ((bf16[128,1,128,384]{3,2,1,0:T(8,128)(2,1)}), bf16[128,1,128,384]{3,2,1,0:T(8,128)(2,1)}, u32[]{:S(2)}, u32[]{:S(2)}) async-start(bf16[128,1,128,384]{3,2,1,0:T(8,128)(2,1)} %bitcast.154), calls=%async_computation | async-start | bytes 25165824 | tf_op jit(solution)/shard_map/all_to_all | solution.py:46
  18.4 0.0 all-gather.2.cloned.1.call-start
  19.2 0.0 copy-done.1
  19.2 0.1 convert_reduce_fusion
  19.3 0.0 copy-done
  19.4 150.7 %all-to-all-done = bf16[128,1,128,384]{3,2,1,0:T(8,128)(2,1)} async-done(((bf16[128,1,128,384]{3,2,1,0:T(8,128)(2,1)}), bf16[128,1,128,384]{3,2,1,0:T(8,128)(2,1)}, u32[]{:S(2)}, u32[]{:S(2)}) %all-to-all-start) | async-done | bytes 12582944 | tf_op jit(solution)/shard_map/all_to_all | solution.py:46
  170.0 14.2 %fusion.22 = f32[384,384]{0,1:T(8,128)S(1)} fusion(bf16[128,1,128,384]{3,2,1,0:T(8,128)(2,1)} %all-to-all-done, bf16[128]{0:T(256)(128)(2,1)S(1)} %convert_element_type.45, f32[]{:T(128)} %bitcast.6), kind=kOutput, calls=%fused_computation.26 | convolution fusion | flops 4838719488 | bytes 13172996 | tf_op jit(solution)/shard_map/bnrd,bnre->bde/dot_general | solution.py:29
  184.2 0.2 copy.17
  184.4 0.1 fusion.27
  184.5 11.7 %custom-call.27 = f32[1,128,128]{2,1,0:T(8,128)S(1)} custom-call(f32[1,128,128]{2,1,0:T(8,128)S(1)} %cholesky.192), custom_call_target="Cholesky" | custom-call | tf_op jit(solution)/shard_map/jit(cholesky)/cholesky | solution.py:34
  196.3 9.8 %custom-call.28 = f32[1,1,128,128]{2,3,1,0:T(8,128)S(1)} custom-call(f32[1,1,128,128]{3,2,1,0:T(8,128)S(1)} %get-tuple-element.29), custom_call_target="InvertDiagBlocksLowerTriangular" | custom-call | tf_op jit(solution)/shard_map/jit(cholesky)/cholesky | solution.py:34
  206.1 0.3 constant_dynamic-update-slice_fusion.2
  206.4 0.3 fusion.10
  206.7 11.7 %custom-call.29 = f32[1,128,128]{2,1,0:T(8,128)S(1)} custom-call(f32[1,128,128]{2,1,0:T(8,128)S(1)} %cholesky.196), custom_call_target="Cholesky" | custom-call | tf_op jit(solution)/shard_map/jit(cholesky)/cholesky | solution.py:34
  218.4 10.0 %custom-call.30 = f32[1,1,128,128]{2,3,1,0:T(8,128)S(1)} custom-call(f32[1,1,128,128]{3,2,1,0:T(8,128)S(1)} %get-tuple-element.26), custom_call_target="InvertDiagBlocksLowerTriangular" | custom-call | tf_op jit(solution)/shard_map/jit(cholesky)/cholesky | solution.py:34
  228.4 0.2 fusion.15
  228.7 0.3 fusion.16
  228.9 11.7 %custom-call.31 = f32[1,128,128]{2,1,0:T(8,128)S(1)} custom-call(f32[1,128,128]{2,1,0:T(8,128)S(1)} %fusion.16), custom_call_target="Cholesky" | custom-call | tf_op jit(solution)/shard_map/jit(cholesky)/cholesky | solution.py:34
  240.7 0.7 compare_reduce_fusion
  241.4 0.7 compare_reduce_fusion.1
  244.0 6.1 %while.1 = (s32[]{:T(128)}, f32[1,384,384]{2,1,0:T(8,128)S(1)}, s32[3,2]{0,1:T(2,128)S(1)}, f32[3,1,128,128]{3,2,1,0:T(8,128)S(1)}, s32[]{:T(128)}) while((s32[]{:T(128)}, f32[1,384,384]{2,1,0:T(8,128)S(1)}, s32[3,2]{0,1:T(2,128)S(1)}, f32[3,1,128,128]{3,2,1,0:T(8,128)S(1)}, s32[]{:T(128)}) %tuple.25), condition=%wide.while_cond, body=%wide.while_body.sunk | while | flops 2 | bytes 131189 | solution.py:20
  244.0 0.1 constant_dynamic-slice_fusion.2
  244.1 0.6 fusion.56
  244.7 1.3 bitcast_dynamic-update-slice_fusion.2
  246.1 0.1 constant_dynamic-slice_fusion.2
  246.2 0.6 fusion.56
  246.8 1.3 bitcast_dynamic-update-slice_fusion.2
  248.1 0.1 constant_dynamic-slice_fusion.2
  248.2 0.6 fusion.56
  248.8 1.3 bitcast_dynamic-update-slice_fusion.2
  250.1 29.5 %custom-call.32 = f32[1,3,128,128]{2,3,1,0:T(8,128)S(1)} custom-call(f32[1,3,128,128]{3,2,1,0:T(8,128)S(1)} %bitcast.162), custom_call_target="InvertDiagBlocksLowerTriangular" | custom-call | tf_op jit(solution)/shard_map/vmap()/triangular_solve | solution.py:20
  279.6 0.3 fusion.33
  279.9 0.3 fusion.12
  280.2 0.3 fusion.39
  280.5 0.3 fusion.14
  280.8 0.3 fusion.41
  281.1 0.3 fusion.40
  281.4 0.3 convolution_subtract_fusion.1
  281.7 0.3 convolution_bitcast_fusion.2
  282.0 0.4 convolution_subtract_fusion
  282.4 0.3 convolution_bitcast_fusion.1
  282.6 0.1 multiply_reduce_fusion
  282.7 0.7 divide_convert_fusion
  283.5 0.0 all-gather.2.cloned.1.call-update
  283.5 110.9 %all-gather.2.cloned.1.call-done = bf16[128,384,256]{2,1,0:T(8,128)(2,1)} async-done(((bf16[1,384,256]{2,1,0:T(8,128)(2,1)}), bf16[128,384,256]{2,1,0:T(8,128)(2,1)}) %all-gather.2.cloned.1.call-update) | async-done | bytes 25165840 | tf_op jit(solution)/shard_map/all_gather | solution.py:54
  394.4 18.0 %convert_bitcast_fusion = bf16[128,128,256]{1,2,0:T(8,128)(2,1)} fusion(bf16[128,384,256]{2,1,0:T(8,128)(2,1)} %all-gather.2.cloned.1.call-done, bf16[128,128,384]{2,1,0:T(8,128)(2,1)} %param.4), kind=kOutput, calls=%fused_computation.6 | convolution fusion | flops 3225419776 | bytes 46137344 | tf_op jit(solution)/shard_map/bgd,bde->bge/dot_general | solution.py:51
  412.4 11.9 %copy.19 = bf16[128,128,256]{2,1,0:T(8,128)(2,1)} copy(bf16[128,128,256]{1,2,0:T(8,128)(2,1)} %convert_bitcast_fusion) | data formatting | bytes 16777216 | tf_op jit(solution)/shard_map/convert_element_type | solution.py:56
  (14 shorter events, 0.3 us)
Async XLA Ops:
  6.5 12.6 %copy-start.1 = (s32[1,128]{1,0:T(1,128)S(1)}, s32[1,128]{1,0:T(1,128)}, u32[]{:S(2)}) copy-start(s32[1,128]{1,0:T(1,128)} %param.6) | copy-start | bytes 1540
  6.5 12.8 %copy-start = (bf16[1,384,256]{2,1,0:T(8,128)(2,1)S(1)}, bf16[1,384,256]{2,1,0:T(8,128)(2,1)}, u32[]{:S(2)}) copy-start(bf16[1,384,256]{2,1,0:T(8,128)(2,1)} %param.5) | copy-start | bytes 589828
  6.5 163.5 %all-to-all-start = ((bf16[128,1,128,384]{3,2,1,0:T(8,128)(2,1)}), bf16[128,1,128,384]{3,2,1,0:T(8,128)(2,1)}, u32[]{:S(2)}, u32[]{:S(2)}) async-start(bf16[128,1,128,384]{3,2,1,0:T(8,128)(2,1)} %bitcast.154), calls=%async_computation | async-start | bytes 25165824 | tf_op jit(solution)/shard_map/all_to_all | solution.py:46
  18.4 375.9 %all-gather.2.cloned.1.call-start = ((), (), s32[]{:S(2)}) async-start(), calls=%async_computation.1 | async-start | bytes 25362432 | tf_op jit(solution)/shard_map/all_gather | solution.py:54
Sparse Core Ops, SparseCore 0:
  283.6 110.7 all-gather.1
where the time goes:
time: 432 us; the launch traced here: 431 us
  waiting for transfers between devices  262 us (61%)
  other arithmetic  87 us (20%)
  matrix products  36.1 us (8%)
  local copies, waits for them, and re-layouts  18.2 us (4%)
  between operations  16.2 us (4%)
  starting transfers between devices  11.9 us (3%)
    all_to_all x1, waiting for transfers between devices, body(): lax.all_to_all(outgoing, ('range', 'doppler'), split_axis=0, concat_axis=...  151 us
    all_gather x1, waiting for transfers between devices, body(): lax.all_gather(weights, ('range', 'doppler'), axis=0, tiled=True)  111 us
    another operation x10, other arithmetic, adapt(): factor = jnp.linalg.cholesky(covariance)  56.4 us
    another operation x3, other arithmetic, solve_one(): lax.linalg.triangular_solve(factor, inner, left_side=True, lower=True, tr...  29.5 us
    dot_general x1, matrix products, body(): jnp.einsum('bgd,bde->bge', snapshots, lax.all_gather(weights, ('range', '...  18 us
    dot_general x1, matrix products, adapt(): jnp.einsum('bnrd,bnre->bde', masked, blocks, preferred_element_type=jnp.f...  14.2 us
    convert_element_type x1, local copies, waits for them, and re-layouts, body(): return jnp.einsum('bgd,bde->bge', snapshots, lax.all_gather(weights, ('ra...  11.9 us
    all_to_all x1, starting transfers between devices, body(): lax.all_to_all(outgoing, ('range', 'doppler'), split_axis=0, concat_axis=...  11.9 us
  transfers between devices with their start and end apart: 2, of which 2 were waited for; matrix products, arithmetic and copies ran while one was open for 0% of the time, Pallas kernels for 0%

commit v1 on v0

--- a/solution.py
+++ b/solution.py
@@ -5,6 +5,11 @@
 
 BLOCK = 128
 LOADING = 0.1
+
+
+def swapped_in(x, axis, along):
+    sent = jnp.stack([x] * lax.axis_size(axis))
+    return jnp.concatenate(lax.all_to_all(sent, axis, 0, 0), axis=along)
 
 
 def selection(train_list, train_count):
@@ -51,7 +56,7 @@
     return jnp.einsum(
         "bgd,bde->bge",
         snapshots,
-        lax.all_gather(weights, ("range", "doppler"), axis=0, tiled=True),
+        swapped_in(weights, ("range", "doppler"), 0),
         preferred_element_type=jnp.float32,
     ).astype(jnp.bfloat16)
 

time: 432 us -> 616 us (1.43)
  blocking collectives: 0 us -> 303 us
  waiting for transfers between devices: 262 us -> 151 us
  between operations: 16.2 us -> 2.82 us
  local copies, waits for them, and re-layouts: 18.2 us -> 24.8 us
    all_to_all x0 -> x1, blocking collectives: none -> 303 us  [swapped_in(): return jnp.concatenate(lax.all_to_all(sent, axis, 0, 0), axis=along)]
    all_gather x1 -> x0, waiting for transfers between devices: 111 us -> none  [body(): lax.all_gather(weights, ('range', 'doppler'), axis=0, tiled=True)]
    another operation x9 -> x10, local copies, waits for them, and re-layouts: 6.04 us -> 12.4 us  [the longest x1 6.37 us: swapped_in(): sent = jnp.stack([x] * lax.axis_size(axis))]
  transfers between devices with their start and end apart: 2 -> 1, of which waited for: 2 -> 1; matrix products, arithmetic and copies ran while one was open for 0% -> 0% of each run, Pallas kernels for 0% -> 0%
where the time goes in v1:
time: 616 us
  blocking collectives  303 us (49%)
  waiting for transfers between devices  151 us (25%)
  other arithmetic  86.3 us (14%)
  matrix products  35.9 us (6%)
  local copies, waits for them, and re-layouts  24.8 us (4%)
  starting transfers between devices  11.9 us (2%)
    all_to_all x1, blocking collectives, swapped_in(): return jnp.concatenate(lax.all_to_all(sent, axis, 0, 0), axis=along)  303 us
    all_to_all x1, waiting for transfers between devices, body(): lax.all_to_all(outgoing, ('range', 'doppler'), split_axis=0, concat_axis=...  151 us
    another operation x10, other arithmetic, adapt(): factor = jnp.linalg.cholesky(covariance)  56.4 us
    another operation x3, other arithmetic, solve_one(): lax.linalg.triangular_solve(factor, inner, left_side=True, lower=True, tr...  29.5 us
    dot_general x1, matrix products, body(): jnp.einsum('bgd,bde->bge', snapshots, swapped_in(weights, ('range', 'dopp...  17.8 us
    dot_general x1, matrix products, adapt(): jnp.einsum('bnrd,bnre->bde', masked, blocks, preferred_element_type=jnp.f...  14.2 us
  transfers between devices with their start and end apart: 1, of which 1 were waited for; matrix products, arithmetic and copies ran while one was open for 0% of the time, Pallas kernels for 0%

profile of v1, /device:TPU:1, one launch (start us, length us, event | category | flops | bytes accessed | tf_op | source)
XLA Modules:
  0.0 615.6 jit_solution(15330382236924793743)
XLA Ops:
  0.0 0.0 copy-start.1
  0.0 0.0 copy-start
  0.0 11.9 %all-to-all-start = ((bf16[128,1,128,384]{3,2,1,0:T(8,128)(2,1)}), bf16[128,1,128,384]{3,2,1,0:T(8,128)(2,1)}, u32[]{:S(2)}, u32[]{:S(2)}) async-start(bf16[128,1,128,384]{3,2,1,0:T(8,128)(2,1)} %bitcast.156), calls=%async_computation | async-start | bytes 25165824 | tf_op jit(solution)/shard_map/all_to_all | solution.py:51
  12.6 0.0 copy-done.1
  12.6 0.1 convert_reduce_fusion
  12.7 0.0 copy-done
  12.8 150.7 %all-to-all-done = bf16[128,1,128,384]{3,2,1,0:T(8,128)(2,1)} async-done(((bf16[128,1,128,384]{3,2,1,0:T(8,128)(2,1)}), bf16[128,1,128,384]{3,2,1,0:T(8,128)(2,1)}, u32[]{:S(2)}, u32[]{:S(2)}) %all-to-all-start) | async-done | bytes 12582944 | tf_op jit(solution)/shard_map/all_to_all | solution.py:51
  163.5 14.2 %fusion.26 = f32[384,384]{0,1:T(8,128)S(1)} fusion(bf16[128,1,128,384]{3,2,1,0:T(8,128)(2,1)} %all-to-all-done, bf16[128]{0:T(256)(128)(2,1)S(1)} %convert_element_type.44, f32[]{:T(128)} %bitcast.6), kind=kOutput, calls=%fused_computation.26 | convolution fusion | flops 4838719488 | bytes 13172996 | tf_op jit(solution)/shard_map/bnrd,bnre->bde/dot_general | solution.py:34
  177.7 0.2 copy.17
  177.9 0.1 fusion.31
  178.0 11.7 %custom-call.27 = f32[1,128,128]{2,1,0:T(8,128)S(1)} custom-call(f32[1,128,128]{2,1,0:T(8,128)S(1)} %cholesky.192), custom_call_target="Cholesky" | custom-call | tf_op jit(solution)/shard_map/jit(cholesky)/cholesky | solution.py:39
  189.7 9.8 %custom-call.28 = f32[1,1,128,128]{2,3,1,0:T(8,128)S(1)} custom-call(f32[1,1,128,128]{3,2,1,0:T(8,128)S(1)} %get-tuple-element.29), custom_call_target="InvertDiagBlocksLowerTriangular" | custom-call | tf_op jit(solution)/shard_map/jit(cholesky)/cholesky | solution.py:39
  199.6 0.3 constant_dynamic-update-slice_fusion.2
  199.9 0.3 fusion.14
  200.2 11.7 %custom-call.29 = f32[1,128,128]{2,1,0:T(8,128)S(1)} custom-call(f32[1,128,128]{2,1,0:T(8,128)S(1)} %cholesky.196), custom_call_target="Cholesky" | custom-call | tf_op jit(solution)/shard_map/jit(cholesky)/cholesky | solution.py:39
  211.9 10.0 %custom-call.30 = f32[1,1,128,128]{2,3,1,0:T(8,128)S(1)} custom-call(f32[1,1,128,128]{3,2,1,0:T(8,128)S(1)} %get-tuple-element.26), custom_call_target="InvertDiagBlocksLowerTriangular" | custom-call | tf_op jit(solution)/shard_map/jit(cholesky)/cholesky | solution.py:39
  221.9 0.2 fusion.19
  222.1 0.3 fusion.20
  222.4 11.7 %custom-call.31 = f32[1,128,128]{2,1,0:T(8,128)S(1)} custom-call(f32[1,128,128]{2,1,0:T(8,128)S(1)} %fusion.20), custom_call_target="Cholesky" | custom-call | tf_op jit(solution)/shard_map/jit(cholesky)/cholesky | solution.py:39
  234.2 0.7 compare_reduce_fusion
  234.9 0.7 compare_reduce_fusion.1
  237.5 6.1 while.1
  237.5 0.1 constant_dynamic-slice_fusion.2
  237.6 0.6 fusion.63
  238.2 1.3 bitcast_dynamic-update-slice_fusion.2
  239.5 0.1 constant_dynamic-slice_fusion.2
  239.6 0.6 fusion.63
  240.2 1.3 bitcast_dynamic-update-slice_fusion.2
  241.6 0.1 constant_dynamic-slice_fusion.2
  241.7 0.6 fusion.63
  242.3 1.3 bitcast_dynamic-update-slice_fusion.2
  243.6 29.5 %custom-call.32 = f32[1,3,128,128]{2,3,1,0:T(8,128)S(1)} custom-call(f32[1,3,128,128]{3,2,1,0:T(8,128)S(1)} %bitcast.166), custom_call_target="InvertDiagBlocksLowerTriangular" | custom-call | tf_op jit(solution)/shard_map/vmap()/triangular_solve | solution.py:25
  273.1 0.3 fusion.39
  273.4 0.3 fusion.16
  273.7 0.3 fusion.47
  274.0 0.3 fusion.18
  274.3 0.3 fusion.49
  274.6 0.3 fusion.48
  274.8 0.3 convolution_subtract_fusion.1
  275.2 0.3 fusion.46
  275.4 0.4 convolution_subtract_fusion
  275.8 0.3 fusion.45
  276.1 0.1 fusion.33
  276.3 0.2 copy.18
  276.4 6.4 %stack.2 = bf16[128,1,384,256]{2,3,1,0:T(8,128)(2,1)S(1)} broadcast(bf16[384,256]{0,1:T(8,128)(2,1)S(1)} %copy.18), dimensions={2,3} | broadcast | bytes 25362432 | tf_op jit(solution)/shard_map/stack | solution.py:11
  282.8 303.1 %all_to_all.10 = bf16[128,1,384,256]{2,3,1,0:T(8,128)(2,1)} all-to-all(bf16[128,1,384,256]{2,3,1,0:T(8,128)(2,1)S(1)} %stack.2), channel_id=1, replica_groups=mesh['range'=16,'doppler'=8] {'range','doppler'}, dimensions={0} | all-to-all | bytes 50331648 | tf_op jit(solution)/shard_map/all_to_all | solution.py:12
  585.9 17.8 %convert_bitcast_fusion = bf16[128,128,256]{1,2,0:T(8,128)(2,1)} fusion(bf16[128,128,384]{2,1,0:T(8,128)(2,1)} %param.4, bf16[128,1,384,256]{2,3,1,0:T(8,128)(2,1)} %all_to_all.10), kind=kOutput, calls=%fused_computation.8 | convolution fusion | flops 3225419776 | bytes 46137344 | tf_op jit(solution)/shard_map/bgd,bde->bge/dot_general | solution.py:56
  603.7 11.9 %copy.19 = bf16[128,128,256]{2,1,0:T(8,128)(2,1)} copy(bf16[128,128,256]{1,2,0:T(8,128)(2,1)} %convert_bitcast_fusion) | data formatting | bytes 16777216 | tf_op jit(solution)/shard_map/convert_element_type | solution.py:61
  (14 shorter events, 0.3 us)
Async XLA Ops:
  0.0 12.6 %copy-start.1 = (s32[1,128]{1,0:T(1,128)S(1)}, s32[1,128]{1,0:T(1,128)}, u32[]{:S(2)}) copy-start(s32[1,128]{1,0:T(1,128)} %param.6) | copy-start | bytes 1540
  0.0 12.7 %copy-start = (bf16[1,384,256]{2,1,0:T(8,128)(2,1)S(1)}, bf16[1,384,256]{2,1,0:T(8,128)(2,1)}, u32[]{:S(2)}) copy-start(bf16[1,384,256]{2,1,0:T(8,128)(2,1)} %param.5) | copy-start | bytes 589828
  0.0 163.5 %all-to-all-start = ((bf16[128,1,128,384]{3,2,1,0:T(8,128)(2,1)}), bf16[128,1,128,384]{3,2,1,0:T(8,128)(2,1)}, u32[]{:S(2)}, u32[]{:S(2)}) async-start(bf16[128,1,128,384]{3,2,1,0:T(8,128)(2,1)} %bitcast.156), calls=%async_computation | async-start | bytes 25165824 | tf_op jit(solution)/shard_map/all_to_all | solution.py:51
